TPU v7x, 32 devices: a whole 2x2x4 slice. The times are simulated.
32 devices in a mesh: dp: 4 (over z), expert: 8 (over y, x, core).
Axes of the slice: x: 2, y: 2, z: 4, core: 2. Of those that a mesh axis runs over, the one named last changes fastest.
Arguments:
- tokens: bfloat16 [8192, 768], P(('dp', 'expert')), may hold values from -6 to 6
- segment_ids: int32 [32, 256], P(('dp', 'expert')), may hold values from 0 to 2, never falling along the last dimension, each value on 1 to 204 neighbouring positions
- routes: int32 [8192, 2], P(('dp', 'expert')), may hold values from 0 to 15, all different within a row
- ln1_gain: float32 [768], P('dp'), may hold values from 0.5 to 1.5
- ln1_bias: float32 [768], P('dp'), may hold values from -0.6 to 0.6
- ln2_gain: float32 [768], P('dp'), may hold values from 0.5 to 1.5
- ln2_bias: float32 [768], P('dp'), may hold values from -0.6 to 0.6
- w_query: float32 [768, 768], P('dp'), may hold values from -0.3125 to 0.3125
- w_key: float32 [768, 768], P('dp'), may hold values from -0.3125 to 0.3125
- w_value: float32 [768, 768], P('dp'), may hold values from -0.21875 to 0.21875
- w_output: float32 [768, 768], P('dp'), may hold values from -0.875 to 0.875
- w_router: float32 [768, 16], P('dp'), may hold values from -0.15625 to 0.15625
- frozen_in: float32 [8, 768, 3072], P('expert', 'dp'), may hold values from -0.21875 to 0.21875
- frozen_out: float32 [8, 3072, 768], P('expert', 'dp'), may hold values from -0.1875 to 0.1875
- new_in: float32 [8, 768, 3072], P('expert', 'dp'), may hold values from -0.21875 to 0.21875
- new_out: float32 [8, 3072, 768], P('expert', 'dp'), may hold values from -0.1875 to 0.1875
- cotangent: bfloat16 [8192, 768], P(('dp', 'expert')), may hold values from -6 to 6
Outputs:
- block_out: bfloat16 [8192, 768], P(('dp', 'expert'))
- grad_tokens: bfloat16 [8192, 768], P(('dp', 'expert'))
- grad_w_query: float32 [768, 768], P('dp')
- grad_w_key: float32 [768, 768], P('dp')
- grad_w_value: float32 [768, 768], P('dp')
- grad_w_output: float32 [768, 768], P('dp')
- grad_w_router: float32 [768, 16], P('dp')
- grad_ln1_gain: float32 [768], P('dp')
- grad_ln1_bias: float32 [768], P('dp')
- grad_ln2_gain: float32 [768], P('dp')
- grad_ln2_bias: float32 [768], P('dp')
- grad_new_in: float32 [8, 768, 3072], P('expert', 'dp')
- grad_new_out: float32 [8, 3072, 768], P('expert', 'dp')
Inputs may be any that keep to these rules, and one draw needn't show every extreme that they name: `segment_ids`: within each row ids never fall, every sequence has 1 to 204 tokens, and one has exactly 204. `routes`: the two experts of a token differ.
All inputs are finite; a program needn't handle non-finite values.
Results may differ from a plain program's by a relative error of at most 0.014.
The roundings to bfloat16 on the way count: a program that leaves them out, or rounds other values in their place, can miss the bound.
Values may be sent and summed in bfloat16 or wider, within the bound.
A program may use at most 192 MiB of HBM per device.

v0:
```python
import jax
import jax.numpy as jnp
from jax import lax
from jax.sharding import PartitionSpec as P

HEADS = 12
HEAD = 64
NORM_EPS = 1e-05
MASKED = -1e30


def layer_norm(values, norm_gain, norm_shift):
    average = jnp.mean(values, axis=-1, keepdims=True)
    centred = values - average
    variance = jnp.mean(centred * centred, axis=-1, keepdims=True)
    return centred * lax.rsqrt(variance + NORM_EPS) * norm_gain + norm_shift


def inner_rows(left, right):
    return lax.dot_general(
        left, right, (((0,), (0,)), ((), ())), preferred_element_type=jnp.float32
    )


def times_transposed(left, right):
    return lax.dot_general(
        left, right, (((1,), (1,)), ((), ())), preferred_element_type=jnp.float32
    )


def shards(
    tokens,
    segment_ids,
    routes,
    ln1_gain,
    ln1_bias,
    ln2_gain,
    ln2_bias,
    w_query,
    w_key,
    w_value,
    w_output,
    w_router,
    frozen_in,
    frozen_out,
    new_in,
    new_out,
    cotangent,
):
    row_count = tokens.shape[0]
    model_width = tokens.shape[1]
    expert_count = w_router.shape[1]
    owner_count = expert_count // 2
    capacity = 5 * row_count // (2 * expert_count)
    slot_count = expert_count * capacity
    score_scale = HEAD ** (-0.5)
    (
        full_query,
        full_key,
        full_value,
        full_output,
        full_router,
        gain_one,
        bias_one,
        gain_two,
        bias_two,
    ) = (
        lax.all_gather(w_query.astype(jnp.bfloat16), "dp", axis=0, tiled=True),
        lax.all_gather(w_key.astype(jnp.bfloat16), "dp", axis=0, tiled=True),
        lax.all_gather(w_value.astype(jnp.bfloat16), "dp", axis=0, tiled=True),
        lax.all_gather(w_output.astype(jnp.bfloat16), "dp", axis=0, tiled=True),
        lax.all_gather(w_router.astype(jnp.bfloat16), "dp", axis=0, tiled=True),
        lax.all_gather(ln1_gain.astype(jnp.bfloat16), "dp", axis=0, tiled=True),
        lax.all_gather(ln1_bias.astype(jnp.bfloat16), "dp", axis=0, tiled=True),
        lax.all_gather(ln2_gain.astype(jnp.bfloat16), "dp", axis=0, tiled=True),
        lax.all_gather(ln2_bias.astype(jnp.bfloat16), "dp", axis=0, tiled=True),
    )
    full_frozen_in, full_frozen_out, full_new_in, full_new_out = (
        lax.all_gather(frozen_in[0].astype(jnp.bfloat16), "dp", axis=0, tiled=True),
        lax.all_gather(frozen_out[0].astype(jnp.bfloat16), "dp", axis=0, tiled=True),
        lax.all_gather(new_in[0].astype(jnp.bfloat16), "dp", axis=0, tiled=True),
        lax.all_gather(new_out[0].astype(jnp.bfloat16), "dp", axis=0, tiled=True),
    )
    stack_in = jnp.stack([full_frozen_in, full_new_in])
    stack_out = jnp.stack([full_frozen_out, full_new_out])
    gain_one_f = gain_one.astype(jnp.float32)
    bias_one_f = bias_one.astype(jnp.float32)
    gain_two_f = gain_two.astype(jnp.float32)
    bias_two_f = bias_two.astype(jnp.float32)
    rows_float = tokens.astype(jnp.float32)
    act_one = layer_norm(rows_float, gain_one_f, bias_one_f).astype(jnp.bfloat16)
    query_rows = jnp.dot(act_one, full_query, preferred_element_type=jnp.float32).astype(
        jnp.bfloat16
    )
    key_rows = jnp.dot(act_one, full_key, preferred_element_type=jnp.float32).astype(jnp.bfloat16)
    value_rows = jnp.dot(act_one, full_value, preferred_element_type=jnp.float32).astype(
        jnp.bfloat16
    )
    query_heads = query_rows.reshape(row_count, HEADS, HEAD)
    key_heads = key_rows.reshape(row_count, HEADS, HEAD)
    value_heads = value_rows.reshape(row_count, HEADS, HEAD)
    segments = segment_ids[0]
    positions = jnp.arange(row_count, dtype=jnp.int32)

    def block_scores(block_index):
        lower = block_index * row_count
        upper_end = lower + row_count
        scores = (
            jnp.einsum("qhd,khd->hqk", query_heads, key_heads, preferred_element_type=jnp.float32)
            * score_scale
        )
        allowed = (segments[lower:upper_end, None] == segments[None, :upper_end]) & (
            positions[None, :upper_end] <= positions[lower:upper_end, None]
        )
        return (jnp.where(allowed[None], scores, MASKED), allowed)

    block_index = 0
    upper_end = (block_index + 1) * row_count
    scores, allowed = block_scores(block_index)
    row_max = jnp.max(scores, axis=-1, keepdims=True)
    expo = jnp.exp(scores - row_max)
    row_total = jnp.sum(expo, axis=-1, keepdims=True)
    probabilities = expo / row_total
    log_totals = [row_max + jnp.log(row_total)]
    attended_parts = jnp.einsum(
        "hqk,khd->qhd",
        probabilities.astype(jnp.bfloat16),
        value_heads,
        preferred_element_type=jnp.float32,
    )
    attended = attended_parts.reshape(row_count, model_width).astype(jnp.bfloat16)
    residual = rows_float + jnp.dot(attended, full_output, preferred_element_type=jnp.float32)
    normed_two = layer_norm(residual, gain_two_f, bias_two_f)
    act_two = normed_two.astype(jnp.bfloat16)
    logits = jnp.dot(act_two, full_router, preferred_element_type=jnp.float32)
    expert_iota = jnp.arange(expert_count, dtype=jnp.int32)
    choose = (routes[:, :, None] == expert_iota[None, None, :]).astype(jnp.float32)
    picked = jnp.sum(choose * logits[:, None, :], axis=2)
    gate_values = jax.nn.softmax(picked, axis=-1)
    flat_ids = routes.reshape(2 * row_count)
    onehot = (flat_ids[:, None] == expert_iota[None, :]).astype(jnp.int32)
    running = jnp.cumsum(onehot, axis=0)
    position = jnp.sum(onehot * running, axis=1) - 1
    is_kept = position < capacity
    kept_float = is_kept.astype(jnp.float32)
    slot_index = (flat_ids % owner_count * 2 + flat_ids // owner_count) * capacity + position
    safe_slot = jnp.where(is_kept, slot_index, 0)
    pair_iota = jnp.arange(2 * row_count, dtype=jnp.int32)
    pair_of_slot = (
        jnp.full((slot_count + 1,), 2 * row_count, jnp.int32)
        .at[jnp.where(is_kept, slot_index, slot_count)]
        .set(pair_iota)[:slot_count]
    )
    token_of_slot = pair_of_slot // 2
    padded_act = jnp.concatenate([act_two, jnp.zeros((1, model_width), jnp.bfloat16)], axis=0)
    dispatched = padded_act[token_of_slot].reshape(owner_count, 2, capacity, model_width)
    received_rows = lax.all_to_all(dispatched, "expert", split_axis=0, concat_axis=0, tiled=True)
    pre_values = jnp.einsum(
        "sekd,edf->sekf", received_rows, stack_in, preferred_element_type=jnp.float32
    )
    hidden = jax.nn.gelu(pre_values).astype(jnp.bfloat16)
    produced_rows = jnp.einsum(
        "sekf,efd->sekd", hidden, stack_out, preferred_element_type=jnp.float32
    ).astype(jnp.bfloat16)
    returned = lax.all_to_all(
        produced_rows, "expert", split_axis=0, concat_axis=0, tiled=True
    ).reshape(slot_count, model_width)
    pair_out = returned[safe_slot].astype(jnp.float32)
    pair_weight = gate_values.reshape(2 * row_count) * kept_float
    mixture = jnp.sum((pair_out * pair_weight[:, None]).reshape(row_count, 2, model_width), axis=1)
    block_out = (residual + mixture).astype(jnp.bfloat16)
    d_out = cotangent.astype(jnp.float32)
    d_out_pairs = jnp.repeat(d_out, 2, axis=0)
    d_gate = kept_float * jnp.sum(pair_out * d_out_pairs, axis=1)
    slot_weight = jnp.concatenate([pair_weight, jnp.zeros((1,), jnp.float32)])[pair_of_slot]
    padded_grad = jnp.concatenate([d_out, jnp.zeros((1, model_width), jnp.float32)], axis=0)
    d_send = (
        (padded_grad[token_of_slot] * slot_weight[:, None])
        .astype(jnp.bfloat16)
        .reshape(owner_count, 2, capacity, model_width)
    )
    again_frozen_in, again_frozen_out, again_new_in, again_new_out = (
        lax.all_gather(frozen_in[0].astype(jnp.bfloat16), "dp", axis=0, tiled=True),
        lax.all_gather(frozen_out[0].astype(jnp.bfloat16), "dp", axis=0, tiled=True),
        lax.all_gather(new_in[0].astype(jnp.bfloat16), "dp", axis=0, tiled=True),
        lax.all_gather(new_out[0].astype(jnp.bfloat16), "dp", axis=0, tiled=True),
    )
    back_in = jnp.stack([again_frozen_in, again_new_in])
    back_out = jnp.stack([again_frozen_out, again_new_out])
    d_produced = lax.all_to_all(d_send, "expert", split_axis=0, concat_axis=0, tiled=True)
    d_hidden = jnp.einsum(
        "sekd,efd->sekf", d_produced, back_out, preferred_element_type=jnp.float32
    )
    gelu_value, gelu_back = jax.vjp(jax.nn.gelu, pre_values)
    d_pre = gelu_back(d_hidden)[0].astype(jnp.bfloat16)
    hidden_again = gelu_value.astype(jnp.bfloat16)
    d_received = jnp.einsum(
        "sekf,edf->sekd", d_pre, back_in, preferred_element_type=jnp.float32
    ).astype(jnp.bfloat16)
    grad_in_full = jnp.einsum(
        "skd,skf->df", received_rows[:, 1], d_pre[:, 1], preferred_element_type=jnp.float32
    )
    grad_out_full = jnp.einsum(
        "skf,skd->fd", hidden_again[:, 1], d_produced[:, 1], preferred_element_type=jnp.float32
    )
    grad_in_part, grad_out_part = (
        lax.psum_scatter(
            grad_in_full.astype(jnp.bfloat16), "dp", scatter_dimension=0, tiled=True
        ).astype(jnp.float32),
        lax.psum_scatter(
            grad_out_full.astype(jnp.bfloat16), "dp", scatter_dimension=0, tiled=True
        ).astype(jnp.float32),
    )
    d_returned = lax.all_to_all(
        d_received, "expert", split_axis=0, concat_axis=0, tiled=True
    ).reshape(slot_count, model_width)
    d_act_moe = jnp.sum(
        (d_returned[safe_slot].astype(jnp.float32) * kept_float[:, None]).reshape(
            row_count, 2, model_width
        ),
        axis=1,
    )
    d_gate_rows = d_gate.reshape(row_count, 2)
    d_picked = gate_values * (
        d_gate_rows - jnp.sum(gate_values * d_gate_rows, axis=1, keepdims=True)
    )
    d_logits = jnp.sum(choose * d_picked[:, :, None], axis=1).astype(jnp.bfloat16)
    grad_router = inner_rows(act_two, d_logits)
    d_act_two = d_act_moe + times_transposed(d_logits, full_router)
    norm_two_value, norm_two_back = jax.vjp(layer_norm, residual, gain_two_f, bias_two_f)
    d_resid_norm, grad_gain_two, grad_bias_two = norm_two_back(d_act_two)
    d_residual = d_out + d_resid_norm
    d_branch = d_residual.astype(jnp.bfloat16)
    grad_output = inner_rows(attended, d_branch)
    d_attended = (
        times_transposed(d_branch, full_output).astype(jnp.bfloat16).reshape(row_count, HEADS, HEAD)
    )
    block_index = 0
    lower = block_index * row_count
    upper_end = lower + row_count
    scores, allowed = block_scores(block_index)
    probabilities = jnp.exp(scores - log_totals[block_index])
    grad_probs = jnp.einsum(
        "qhd,khd->hqk", d_attended, value_heads, preferred_element_type=jnp.float32
    )
    row_delta = jnp.sum(grad_probs * probabilities, axis=-1, keepdims=True)
    grad_scores = jnp.where(allowed[None], probabilities * (grad_probs - row_delta), 0.0).astype(
        jnp.bfloat16
    )
    d_query_parts = (
        jnp.einsum("hqk,khd->qhd", grad_scores, key_heads, preferred_element_type=jnp.float32)
        * score_scale
    )
    d_key_sum = (
        jnp.einsum("hqk,qhd->khd", grad_scores, query_heads, preferred_element_type=jnp.float32)
        * score_scale
    )
    d_value_sum = jnp.einsum(
        "hqk,qhd->khd",
        probabilities.astype(jnp.bfloat16),
        d_attended,
        preferred_element_type=jnp.float32,
    )
    d_query = d_query_parts.reshape(row_count, model_width).astype(jnp.bfloat16)
    d_key = d_key_sum.reshape(row_count, model_width).astype(jnp.bfloat16)
    d_value = d_value_sum.reshape(row_count, model_width).astype(jnp.bfloat16)
    grad_query = inner_rows(act_one, d_query)
    grad_key = inner_rows(act_one, d_key)
    grad_value = inner_rows(act_one, d_value)
    d_act_one = (
        times_transposed(d_query, full_query)
        + times_transposed(d_key, full_key)
        + times_transposed(d_value, full_value)
    )
    norm_one_value, norm_one_back = jax.vjp(layer_norm, rows_float, gain_one_f, bias_one_f)
    d_rows_norm, grad_gain_one, grad_bias_one = norm_one_back(d_act_one)
    grad_tokens = (d_residual + d_rows_norm).astype(jnp.bfloat16)
    summed = lax.psum(
        (
            grad_query,
            grad_key,
            grad_value,
            grad_output,
            grad_router,
            grad_gain_one,
            grad_bias_one,
            grad_gain_two,
            grad_bias_two,
        ),
        ("dp", "expert"),
    )
    share_rows = model_width // lax.axis_size("dp")
    offset = lax.axis_index("dp") * share_rows
    shares = tuple((lax.dynamic_slice_in_dim(member, offset, share_rows, 0) for member in summed))
    return (
        block_out,
        grad_tokens,
        shares[0],
        shares[1],
        shares[2],
        shares[3],
        shares[4],
        shares[5],
        shares[6],
        shares[7],
        shares[8],
        grad_in_part[None],
        grad_out_part[None],
    )


def solution(mesh):
    in_specs = (
        P(("dp", "expert"), None),
        P(("dp", "expert"), None),
        P(("dp", "expert"), None),
        P("dp"),
        P("dp"),
        P("dp"),
        P("dp"),
        P("dp", None),
        P("dp", None),
        P("dp", None),
        P("dp", None),
        P("dp", None),
        P("expert", "dp", None),
        P("expert", "dp", None),
        P("expert", "dp", None),
        P("expert", "dp", None),
        P(("dp", "expert"), None),
    )
    out_specs = (
        P(("dp", "expert"), None),
        P(("dp", "expert"), None),
        P("dp", None),
        P("dp", None),
        P("dp", None),
        P("dp", None),
        P("dp", None),
        P("dp"),
        P("dp"),
        P("dp"),
        P("dp"),
        P("expert", "dp", None),
        P("expert", "dp", None),
    )
    return jax.shard_map(shards, mesh=mesh, in_specs=in_specs, out_specs=out_specs, check_vma=False)
```

profile of v0, /device:TPU:0, one launch (start us, length us, event | category | flops | bytes accessed | tf_op | source)
XLA Modules:
  0.0 1022.0 jit_solution(8854546606733937688)
XLA Ops:
  27.9 14.3 %all-reduce.8 = (bf16[768]{0:T(1024)(128)(2,1)S(1)}, bf16[768]{0:T(1024)(128)(2,1)S(1)}, bf16[768]{0:T(1024)(128)(2,1)S(1)}, bf16[768]{0:T(1024)(128)(2,1)S(1)}) all-reduce(bf16[768]{0:T(1024)(128)(2,1)S(1)} %dynamic-update-slice.1, bf16[768]{0:T(1024)(128)(2,1)S(1)} %dynamic-update-slice, ...), channel_id=1, replica_groups=mesh['dp'=4,'expert'=8] {'dp'}, use_global_device_ids=true, to_apply=%add.3 | all-reduce | flops 3072 | bytes 12288
  48.0 27.4 %all-gather.18.cloned.1.call-done = bf16[768,768]{1,0:T(8,128)(2,1)} async-done(((bf16[192,768]{1,0:T(8,128)(2,1)}), bf16[768,768]{1,0:T(8,128)(2,1)}) %all-gather.18.cloned.1.call-update) | async-done | bytes 1179664 | tf_op jit(solution)/shard_map/all_gather | solution.py:69
  77.4 29.7 %all-gather.16.cloned.1.call-done = bf16[768,768]{1,0:T(8,128)(2,1)} async-done(((bf16[192,768]{1,0:T(8,128)(2,1)}), bf16[768,768]{1,0:T(8,128)(2,1)}) %all-gather.16.cloned.1.call-update) | async-done | bytes 1179664 | tf_op jit(solution)/shard_map/all_gather | solution.py:68
  112.2 26.4 %all-gather.20.cloned.1.call-done = bf16[768,768]{1,0:T(8,128)(2,1)} async-done(((bf16[192,768]{1,0:T(8,128)(2,1)}), bf16[768,768]{1,0:T(8,128)(2,1)}) %all-gather.20.cloned.1.call-update) | async-done | bytes 1179664 | tf_op jit(solution)/shard_map/all_gather | solution.py:71
  145.6 18.3 %all_to_all.20 = bf16[8,2,40,768]{3,2,1,0:T(8,128)(2,1)S(1)} all-to-all(bf16[8,2,40,768]{3,2,1,0:T(8,128)(2,1)S(1)} %bitcast.156), channel_id=1, replica_groups=mesh['dp'=4,'expert'=8] {'expert'}, dimensions={0} | all-to-all | bytes 1966080 | tf_op jit(solution)/shard_map/all_to_all | solution.py:157
  163.8 65.4 %all-gather.26.cloned.1.call-done = bf16[1,768,3072]{2,1,0:T(8,128)(2,1)} async-done(((bf16[1,192,3072]{2,1,0:T(8,128)(2,1)}), bf16[1,768,3072]{2,1,0:T(8,128)(2,1)}) %all-gather.26.cloned.1.call-update) | async-done | bytes 4718608 | tf_op jit(solution)/shard_map/all_gather | solution.py:79
  229.3 89.8 %all-gather.28.cloned.1.call-done = bf16[1,768,3072]{2,1,0:T(8,128)(2,1)} async-done(((bf16[1,192,3072]{2,1,0:T(8,128)(2,1)}), bf16[1,768,3072]{2,1,0:T(8,128)(2,1)}) %all-gather.28.cloned.1.call-update) | async-done | bytes 4718608 | tf_op jit(solution)/shard_map/all_gather | solution.py:81
  319.1 9.6 fusion.11
  328.7 79.8 %all-gather.22.cloned.1.call-done = bf16[1,3072,768]{2,1,0:T(8,128)(2,1)} async-done(((bf16[1,768,768]{2,1,0:T(8,128)(2,1)}), bf16[1,3072,768]{2,1,0:T(8,128)(2,1)}) %all-gather.22.cloned.1.call-update) | async-done | bytes 4718608 | tf_op jit(solution)/shard_map/all_gather | solution.py:80
  408.5 89.4 %all-gather.24.cloned.1.call-done = bf16[1,3072,768]{2,1,0:T(8,128)(2,1)} async-done(((bf16[1,768,768]{2,1,0:T(8,128)(2,1)}), bf16[1,3072,768]{2,1,0:T(8,128)(2,1)}) %all-gather.24.cloned.1.call-update) | async-done | bytes 4718608 | tf_op jit(solution)/shard_map/all_gather | solution.py:82
  497.9 8.1 fusion.42
  507.1 3.7 all-to-all-start.1
  510.7 13.1 %all-gather.4 = bf16[4,192,16]{1,2,0:T(8,128)(2,1)S(1)} all-gather(bf16[1,192,16]{1,2,0:T(8,128)(2,1)S(1)} %convert_bitcast_fusion), channel_id=1, replica_groups=mesh['dp'=4,'expert'=8] {'dp'}, dimensions={0}, use_global_device_ids=true | all-gather | bytes 30720 | tf_op jit(solution)/shard_map/all_gather | solution.py:72
  525.6 3.3 gather_fusion.2
  546.7 4.6 gather_fusion.3
  552.3 19.1 %all_to_all.21 = bf16[8,2,40,768]{3,2,1,0:T(8,128)(2,1)S(1)} all-to-all(bf16[8,2,40,768]{3,2,1,0:T(8,128)(2,1)S(1)} %multiply_convert_fusion), channel_id=1, replica_groups=mesh['dp'=4,'expert'=8] {'expert'}, dimensions={0} | all-to-all | bytes 1966080 | tf_op jit(solution)/shard_map/all_to_all | solution.py:190
  572.3 12.5 %fusion.7 = bf16[8,2,40,3072]{3,2,0,1:T(8,128)(2,1)} fusion(f32[2,3072,8,40]{1,3,2,0:T(8,128)} %get-tuple-element.49, bf16[1,3072,768]{2,1,0:T(8,128)(2,1)} %all-gather.24.cloned.1.call-done, bf16[1,3072,768]{2,1,0:T(8,128)(2,1)} %all-gather.22.cloned.1.call-done, bf16[8,2,40,768]{3,2,1,0:T(8,128)(2,1)S(1)} %all_to_all.21), kind=kOutput, calls=%fused_computation.19 | convolution fusion | flops 3078094848 | bytes 22216704 | tf_op jit(solution)/shard_map/sekd,efd->sekf/dot_general | solution.py:191
  584.8 6.9 fusion.41
  592.8 3.6 all-to-all-start.3
  600.5 4.3 multiply_reduce_fusion.3
  604.7 6.2 all-to-all-done.3
  611.0 3.2 gather_fusion.4
  625.7 3.4 fusion.114
  630.5 4.9 fusion.56
  635.4 5.0 fusion.53
  640.4 3.2 fusion.99
  649.0 6.6 bitcast_convert_fusion.1
  656.8 6.5 bitcast_convert_fusion
  670.7 38.8 %all-reduce.6 = (f32[768,16]{0,1:T(8,128)S(1)}, f32[768]{0:T(1024)S(1)}, f32[768]{0:T(1024)S(1)}, f32[768]{0:T(1024)S(1)}, f32[768]{0:T(1024)S(1)}) all-reduce(f32[768,16]{0,1:T(8,128)S(1)} %fusion.116, f32[768]{0:T(1024)S(1)} %get-tuple-element.15, ...), channel_id=1, replica_groups=mesh['dp'=4,'expert'=8] {'dp','expert'}, use_global_device_ids=true, to_apply=%region_27.28 | all-reduce | flops 15360 | bytes 122880 | tf_op jit(solution)/shard_map/psum | solution.py:278
  713.9 122.9 %all-reduce.11.cloned.1.call-done = (f32[768,768]{1,0:T(8,128)}, f32[768,768]{1,0:T(8,128)}, f32[768,768]{1,0:T(8,128)}, f32[768,768]{1,0:T(8,128)}) async-done(((f32[768,768]{1,0:T(8,128)}, f32[768,768]{1,0:T(8,128)}, f32[768,768]{1,0:T(8,128)}, f32[768,768]{1,0:T(8,128)}), (f32[768,768]{1,0:T(8,128)}, f32[768,768]{1,0:T(8,128)}, f32[768,768]{1,0:T(8,128)}, ...) | async-done | bytes 9437200 | tf_op jit(solution)/shard_map/psum | solution.py:278
  844.5 79.9 %reduce-scatter.3.cloned.1.call-done = bf16[192,3072]{1,0:T(8,128)(2,1)} async-done(((bf16[768,3072]{1,0:T(8,128)(2,1)}), bf16[192,3072]{1,0:T(8,128)(2,1)}) %reduce-scatter.3.cloned.1.call-update) | async-done | bytes 1179664 | tf_op jit(solution)/shard_map/reduce_scatter | solution.py:207
  927.2 85.2 %reduce-scatter.5.cloned.1.call-done = bf16[768,768]{1,0:T(8,128)(2,1)} async-done(((bf16[3072,768]{1,0:T(8,128)(2,1)}), bf16[768,768]{1,0:T(8,128)(2,1)}) %reduce-scatter.5.cloned.1.call-update) | async-done | bytes 1179664 | tf_op jit(solution)/shard_map/reduce_scatter | solution.py:210
  (314 shorter events, 111.2 us)
Async XLA Ops:
  7.2 38.8 %all-gather.14.cloned.1.call-start = ((), (), s32[]{:S(2)}) async-start(), calls=%async_computation.6 | async-start | bytes 1474560 | tf_op jit(solution)/shard_map/all_gather | solution.py:70
  9.2 66.2 %all-gather.18.cloned.1.call-start = ((), (), s32[]{:S(2)}) async-start(), calls=%async_computation.8 | async-start | bytes 1474560 | tf_op jit(solution)/shard_map/all_gather | solution.py:69
  11.1 96.0 %all-gather.16.cloned.1.call-start = ((), (), s32[]{:S(2)}) async-start(), calls=%async_computation.7 | async-start | bytes 1474560 | tf_op jit(solution)/shard_map/all_gather | solution.py:68
  13.0 125.6 %all-gather.20.cloned.1.call-start = ((), (), s32[]{:S(2)}) async-start(), calls=%async_computation.9 | async-start | bytes 1474560 | tf_op jit(solution)/shard_map/all_gather | solution.py:71
  13.8 215.4 %all-gather.26.cloned.1.call-start = ((), (), s32[]{:S(2)}) async-start(), calls=%async_computation.14 | async-start | bytes 5898240 | tf_op jit(solution)/shard_map/all_gather | solution.py:79
  15.1 304.0 %all-gather.28.cloned.1.call-start = ((), (), s32[]{:S(2)}) async-start(), calls=%async_computation.15 | async-start | bytes 5898240 | tf_op jit(solution)/shard_map/all_gather | solution.py:81
  18.1 390.3 %all-gather.22.cloned.1.call-start = ((), (), s32[]{:S(2)}) async-start(), calls=%async_computation.12 | async-start | bytes 5898240 | tf_op jit(solution)/shard_map/all_gather | solution.py:80
  19.4 26.1 %copy-start = (bf16[256,768]{1,0:T(8,128)(2,1)S(1)}, bf16[256,768]{1,0:T(8,128)(2,1)}, u32[]{:S(2)}) copy-start(bf16[256,768]{1,0:T(8,128)(2,1)} %param.17) | copy-start | bytes 1179652
  19.4 26.5 %copy-start.73 = (s32[1,256]{1,0:T(1,128)S(1)}, s32[1,256]{1,0:T(1,128)}, u32[]{:S(2)}) copy-start(s32[1,256]{1,0:T(1,128)} %param.18) | copy-start | bytes 3076
  19.4 478.5 %all-gather.24.cloned.1.call-start = ((), (), s32[]{:S(2)}) async-start(), calls=%async_computation.13 | async-start | bytes 5898240 | tf_op jit(solution)/shard_map/all_gather | solution.py:82
  42.3 64.8 %copy-start.40 = (f32[768]{0:T(1024)}, f32[768]{0:T(1024)S(1)}, u32[]{:S(2)}) copy-start(f32[768]{0:T(1024)S(1)} %convert_element_type.216) | copy-start | bytes 9220
  42.3 98.4 %copy-start.42 = (f32[768]{0:T(1024)}, f32[768]{0:T(1024)S(1)}, u32[]{:S(2)}) copy-start(f32[768]{0:T(1024)S(1)} %convert_element_type.238) | copy-start | bytes 9220
  45.4 97.2 %copy-start.49 = (s32[1024]{0:T(1024)}, s32[1024]{0:T(1024)S(1)}, u32[]{:S(2)}) copy-start(s32[1024]{0:T(1024)S(1)} %get-tuple-element.53) | copy-start | bytes 12292
  45.6 61.5 %copy-start.38 = (f32[256]{0:T(256)}, f32[256]{0:T(256)S(1)}, u32[]{:S(2)}) copy-start(f32[256]{0:T(256)S(1)} %broadcast_multiply_fusion.1) | copy-start | bytes 3076
  45.8 31.6 %copy-start.66 = (f32[256]{0:T(256)}, f32[256]{0:T(256)S(1)}, u32[]{:S(2)}) copy-start(f32[256]{0:T(256)S(1)} %fusion.68) | copy-start | bytes 3076
  45.9 61.2 %copy-start.47 = (f32[256]{0:T(256)}, f32[256]{0:T(256)S(1)}, u32[]{:S(2)}) copy-start(f32[256]{0:T(256)S(1)} %fusion.88) | copy-start | bytes 3076
  46.0 63.1 %copy-start.33 = (pred[256,256]{0,1:T(8,128)(4,1)}, pred[256,256]{0,1:T(8,128)(4,1)S(1)}, u32[]{:S(2)}) copy-start(pred[256,256]{0,1:T(8,128)(4,1)S(1)} %fusion.70) | copy-start | bytes 196612
  48.0 62.3 %copy-start.23 = (bf16[256,768]{0,1:T(8,128)(2,1)}, bf16[256,768]{0,1:T(8,128)(2,1)S(1)}, u32[]{:S(2)}) copy-start(bf16[256,768]{0,1:T(8,128)(2,1)S(1)} %copy.85) | copy-start | bytes 1179652
  77.4 32.4 %copy-start.24 = (bf16[256,768]{0,1:T(8,128)(2,1)}, bf16[256,768]{0,1:T(8,128)(2,1)S(1)}, u32[]{:S(2)}) copy-start(bf16[256,768]{0,1:T(8,128)(2,1)S(1)} %copy.87) | copy-start | bytes 1179652
  112.2 28.5 %copy-start.19 = (bf16[12,64,256]{2,1,0:T(8,128)(2,1)}, bf16[12,64,256]{2,1,0:T(8,128)(2,1)S(1)}, u32[]{:S(2)}) copy-start(bf16[12,64,256]{2,1,0:T(8,128)(2,1)S(1)} %fusion.49) | copy-start | bytes 1179652
  163.8 164.9 %copy-start.26 = (bf16[8,2,40,768]{3,2,1,0:T(8,128)(2,1)}, bf16[8,2,40,768]{3,2,1,0:T(8,128)(2,1)S(1)}, u32[]{:S(2)}) copy-start(bf16[8,2,40,768]{3,2,1,0:T(8,128)(2,1)S(1)} %all_to_all.20) | copy-start | bytes 2949124
  506.0 19.5 %copy-start.5 = (bf16[256,768]{1,0:T(8,128)(2,1)S(1)}, bf16[256,768]{1,0:T(8,128)(2,1)}, u32[]{:S(2)}) copy-start(bf16[256,768]{1,0:T(8,128)(2,1)} %param.33) | copy-start | bytes 1179652
  506.0 19.5 %copy-start.50 = (s32[1024]{0:T(1024)S(1)}, s32[1024]{0:T(1024)}, u32[]{:S(2)}) copy-start(s32[1024]{0:T(1024)} %copy-done.49) | copy-start | bytes 12292
  507.1 27.5 %all-to-all-start.1 = ((bf16[8,2,40,768]{3,2,1,0:T(8,128)(2,1)}), bf16[8,2,40,768]{3,2,1,0:T(8,128)(2,1)S(1)}, u32[]{:S(2)}, u32[]{:S(2)}) async-start(bf16[8,2,40,768]{3,2,1,0:T(8,128)(2,1)} %copy.94), calls=%async_computation.1 | async-start | bytes 1966080 | tf_op jit(solution)/shard_map/all_to_all | solution.py:165
  552.1 32.8 %slice-start = ((s8[4718592]{0:T(1024)(128)(4,1)}), s8[4194304]{0:T(1024)(128)(4,1)S(1)}, s32[]{:S(2)}) async-start(s8[4718592]{0:T(1024)(128)(4,1)} %bitcast.178), calls=%async_computation.17 | async-start | bytes 8388608
  592.8 18.2 %all-to-all-start.3 = ((bf16[8,2,40,768]{3,2,1,0:T(8,128)(2,1)}), bf16[8,2,40,768]{3,2,1,0:T(8,128)(2,1)S(1)}, u32[]{:S(2)}, u32[]{:S(2)}) async-start(bf16[8,2,40,768]{3,2,1,0:T(8,128)(2,1)} %copy.100), calls=%async_computation.3 | async-start | bytes 1966080 | tf_op jit(solution)/shard_map/all_to_all | solution.py:214
  596.4 240.4 %all-reduce.11.cloned.1.call-start = ((), (), s32[]{:S(2)}) async-start(), calls=%async_computation.16 | async-start | bytes 18874368 | tf_op jit(solution)/shard_map/psum | solution.py:278
  647.8 276.5 %reduce-scatter.3.cloned.1.call-start = ((), (), s32[]{:S(2)}) async-start(), calls=%async_computation.10 | async-start | bytes 5898240 | tf_op jit(solution)/shard_map/reduce_scatter | solution.py:207
  655.6 356.9 %reduce-scatter.5.cloned.1.call-start = ((), (), s32[]{:S(2)}) async-start(), calls=%async_computation.11 | async-start | bytes 5898240 | tf_op jit(solution)/shard_map/reduce_scatter | solution.py:210
  668.2 44.6 %copy-start.4 = (f32[256,768]{1,0:T(8,128)S(1)}, f32[256,768]{1,0:T(8,128)}, u32[]{:S(2)}) copy-start(f32[256,768]{1,0:T(8,128)} %copy-done.3) | copy-start | bytes 2359300
  668.2 44.6 %copy-start.7 = (bf16[256,768]{1,0:T(8,128)(2,1)S(1)}, bf16[256,768]{1,0:T(8,128)(2,1)}, u32[]{:S(2)}) copy-start(bf16[256,768]{1,0:T(8,128)(2,1)} %param.33) | copy-start | bytes 1179652
  668.2 44.6 %copy-start.59 = (f32[256]{0:T(256)S(1)}, f32[256]{0:T(256)}, u32[]{:S(2)}) copy-start(f32[256]{0:T(256)} %copy-done.58) | copy-start | bytes 3076
  (62 other events, 265.4 us)
Sparse Core Ops, SparseCore 0:
  10.1 33.5 all-gather.13
  45.8 29.5 all-gather.17
  77.6 29.4 all-gather.15
  109.1 29.4 all-gather.19
  140.6 88.6 all-gather.25
  231.3 87.7 all-gather.27
  320.7 87.7 all-gather.21
  410.1 87.7 all-gather.23
  647.9 188.8 all-reduce.10
  838.9 85.3 reduce-scatter.2
  926.6 85.7 reduce-scatter.4
where the time goes:
time: 1030 us; the launch traced here: 1020 us
  waiting for transfers between devices  702 us (68%)
  blocking collectives  104 us (10%)
  matrix products  91.2 us (9%)
  local copies, waits for them, and re-layouts  61 us (6%)
  other arithmetic  40.4 us (4%)
  between operations  15.9 us (2%)
    psum x1, waiting for transfers between devices, shards(): lax.psum((grad_query, grad_key, grad_value, grad_output, grad_router, gra...  123 us
    all_gather x1, waiting for transfers between devices, shards(): lax.all_gather(new_in[0].astype(jnp.bfloat16), 'dp', axis=0, tiled=True)  89.8 us
    all_gather x1, waiting for transfers between devices, shards(): lax.all_gather(new_out[0].astype(jnp.bfloat16), 'dp', axis=0, tiled=True)  89.4 us
    reduce_scatter x1, waiting for transfers between devices, shards(): lax.psum_scatter(grad_out_full.astype(jnp.bfloat16), 'dp', scatter_dimens...  85.2 us
    reduce_scatter x1, waiting for transfers between devices, shards(): lax.psum_scatter(grad_in_full.astype(jnp.bfloat16), 'dp', scatter_dimensi...  79.9 us
    all_gather x1, waiting for transfers between devices, shards(): lax.all_gather(frozen_out[0].astype(jnp.bfloat16), 'dp', axis=0, tiled=True)  79.8 us
    all_gather x1, waiting for transfers between devices, shards(): lax.all_gather(frozen_in[0].astype(jnp.bfloat16), 'dp', axis=0, tiled=True)  65.4 us
    psum x1, blocking collectives, shards(): lax.psum((grad_query, grad_key, grad_value, grad_output, grad_router, gra...  38.8 us
  transfers between devices with their start and end apart: 13, of which 11 were waited for; matrix products, arithmetic and copies ran while one was open for 9% of the time, Pallas kernels for 0%

commit v1 on v0

--- a/solution.py
+++ b/solution.py
@@ -7,6 +7,32 @@
 HEAD = 64
 NORM_EPS = 1e-05
 MASKED = -1e30
+
+
+def form_masks_over_axis(load, dim_k):
+    r2 = list(load.shape[1:])
+    r2[dim_k] *= load.shape[0]
+    h_now = jnp.moveaxis(load, 0, dim_k).reshape(r2)
+    return h_now
+
+
+def advance_members_all(original, along_axis):
+    n_blocks = lax.axis_size(along_axis)
+    y_new = original[None]
+    for t in range(n_blocks.bit_length() - 1):
+        state_now = 1 << t
+        piece_next = lax.ppermute(
+            y_new, along_axis, list(map(lambda pp: (pp, pp ^ state_now), range(n_blocks)))
+        )
+        carry_out = jnp.stack([y_new, piece_next], axis=0)
+        d_next = lax.axis_index(along_axis) >> t & 1
+        y_new = jnp.where(d_next == 0, carry_out, carry_out[::-1]).reshape(-1, *original.shape)
+    return y_new
+
+
+def read_types_by_axis(sheet, point, at_axis):
+    wide_out = form_masks_over_axis(advance_members_all(sheet, point), at_axis)
+    return wide_out
 
 
 def layer_norm(values, norm_gain, norm_shift):
@@ -77,7 +103,7 @@
     )
     full_frozen_in, full_frozen_out, full_new_in, full_new_out = (
         lax.all_gather(frozen_in[0].astype(jnp.bfloat16), "dp", axis=0, tiled=True),
-        lax.all_gather(frozen_out[0].astype(jnp.bfloat16), "dp", axis=0, tiled=True),
+        read_types_by_axis(frozen_out[0].astype(jnp.bfloat16), "dp", 0),
         lax.all_gather(new_in[0].astype(jnp.bfloat16), "dp", axis=0, tiled=True),
         lax.all_gather(new_out[0].astype(jnp.bfloat16), "dp", axis=0, tiled=True),
     )

time: 1030 us -> 1060 us (1.029)
  waiting for transfers between devices: 702 us -> 735 us
  starting transfers between devices: 7.68 us -> 20.2 us
  blocking collectives: 104 us -> 91.7 us
  local copies, waits for them, and re-layouts: 61 us -> 49.5 us
    all_gather x1, waiting for transfers between devices: 79.8 us -> 39.7 us  [shards(): lax.all_gather(frozen_out[0].astype(jnp.bfloat16), 'dp', axis=0, tiled=True)]
    all_gather x1, waiting for transfers between devices: 27.4 us -> 67.2 us  [shards(): lax.all_gather(w_key.astype(jnp.bfloat16), 'dp', axis=0, tiled=True)]
    all_gather x1, waiting for transfers between devices: 0.02 us -> 39.1 us  [shards(): lax.all_gather(w_value.astype(jnp.bfloat16), 'dp', axis=0, tiled=True)]
    all_to_all x2 -> x0, blocking collectives: 37.4 us -> none  [the longest x1 19.1 us: shards(): lax.all_to_all(d_send, 'expert', split_axis=0, concat_axis=0, tiled=True)]
    all_gather x1, waiting for transfers between devices: 29.7 us -> 0.01 us  [shards(): lax.all_gather(w_query.astype(jnp.bfloat16), 'dp', axis=0, tiled=True)]
    unnamed x1, blocking collectives: 14.3 us -> 38.3 us
    all_gather x1, waiting for transfers between devices: 26.4 us -> 49.3 us  [shards(): lax.all_gather(w_output.astype(jnp.bfloat16), 'dp', axis=0, tiled=True)]
  transfers between devices with their start and end apart: 13 -> 17, of which waited for: 11 -> 12; matrix products, arithmetic and copies ran while one was open for 9% -> 12% of each run, Pallas kernels for 0% -> 0%
where the time goes in v1:
time: 1060 us; the launch traced here: 1050 us
  waiting for transfers between devices  735 us (69%)
  matrix products  93.1 us (9%)
  blocking collectives  91.7 us (9%)
  local copies, waits for them, and re-layouts  49.5 us (5%)
  other arithmetic  48.2 us (5%)
  starting transfers between devices  20.2 us (2%)
  between operations  15.9 us (2%)
    psum x1, waiting for transfers between devices, shards(): lax.psum((grad_query, grad_key, grad_value, grad_output, grad_router, gra...  124 us
    all_gather x1, waiting for transfers between devices, shards(): lax.all_gather(new_in[0].astype(jnp.bfloat16), 'dp', axis=0, tiled=True)  89.3 us
    reduce_scatter x1, waiting for transfers between devices, shards(): lax.psum_scatter(grad_in_full.astype(jnp.bfloat16), 'dp', scatter_dimensi...  85.3 us
    reduce_scatter x1, waiting for transfers between devices, shards(): lax.psum_scatter(grad_out_full.astype(jnp.bfloat16), 'dp', scatter_dimens...  79.9 us
    all_gather x1, waiting for transfers between devices, shards(): lax.all_gather(new_out[0].astype(jnp.bfloat16), 'dp', axis=0, tiled=True)  79.6 us
    all_gather x1, waiting for transfers between devices, shards(): lax.all_gather(w_key.astype(jnp.bfloat16), 'dp', axis=0, tiled=True)  67.2 us
    all_gather x1, waiting for transfers between devices, shards(): lax.all_gather(frozen_in[0].astype(jnp.bfloat16), 'dp', axis=0, tiled=True)  65 us
    all_gather x1, waiting for transfers between devices, shards(): lax.all_gather(w_output.astype(jnp.bfloat16), 'dp', axis=0, tiled=True)  49.3 us
  transfers between devices with their start and end apart: 17, of which 12 were waited for; matrix products, arithmetic and copies ran while one was open for 12% of the time, Pallas kernels for 0%

profile of v1, /device:TPU:0, one launch (start us, length us, event | category | flops | bytes accessed | tf_op | source)
XLA Modules:
  0.0 1053.8 jit_solution(1341494153366915793)
XLA Ops:
  33.7 38.3 %all-reduce.8 = (bf16[768]{0:T(1024)(128)(2,1)S(1)}, bf16[768]{0:T(1024)(128)(2,1)S(1)}, bf16[768]{0:T(1024)(128)(2,1)S(1)}, bf16[768]{0:T(1024)(128)(2,1)S(1)}) all-reduce(bf16[768]{0:T(1024)(128)(2,1)S(1)} %dynamic-update-slice.1, bf16[768]{0:T(1024)(128)(2,1)S(1)} %dynamic-update-slice, ...), channel_id=1, replica_groups=mesh['dp'=4,'expert'=8] {'dp'}, use_global_device_ids=true, to_apply=%add.3 | all-reduce | flops 3072 | bytes 12288
  78.8 67.2 %all-gather.18.cloned.1.call-done = bf16[768,768]{1,0:T(8,128)(2,1)} async-done(((bf16[192,768]{1,0:T(8,128)(2,1)}), bf16[768,768]{1,0:T(8,128)(2,1)}) %all-gather.18.cloned.1.call-update) | async-done | bytes 1179664 | tf_op jit(solution)/shard_map/all_gather | solution.py:95
  148.0 39.1 %all-gather.14.cloned.1.call-done = bf16[768,768]{1,0:T(8,128)(2,1)} async-done(((bf16[192,768]{1,0:T(8,128)(2,1)}), bf16[768,768]{1,0:T(8,128)(2,1)}) %all-gather.14.cloned.1.call-update) | async-done | bytes 1179664 | tf_op jit(solution)/shard_map/all_gather | solution.py:96
  192.2 49.3 %all-gather.20.cloned.1.call-done = bf16[768,768]{1,0:T(8,128)(2,1)} async-done(((bf16[192,768]{1,0:T(8,128)(2,1)}), bf16[768,768]{1,0:T(8,128)(2,1)}) %all-gather.20.cloned.1.call-update) | async-done | bytes 1179664 | tf_op jit(solution)/shard_map/all_gather | solution.py:97
  244.6 3.4 gather_fusion
  248.0 3.9 all-to-all-start
  258.1 8.5 all-to-all-done
  266.5 65.0 %all-gather.24.cloned.1.call-done = bf16[1,768,3072]{2,1,0:T(8,128)(2,1)} async-done(((bf16[1,192,3072]{2,1,0:T(8,128)(2,1)}), bf16[1,768,3072]{2,1,0:T(8,128)(2,1)}) %all-gather.24.cloned.1.call-update) | async-done | bytes 4718608 | tf_op jit(solution)/shard_map/all_gather | solution.py:105
  331.6 89.3 %all-gather.26.cloned.1.call-done = bf16[1,768,3072]{2,1,0:T(8,128)(2,1)} async-done(((bf16[1,192,3072]{2,1,0:T(8,128)(2,1)}), bf16[1,768,3072]{2,1,0:T(8,128)(2,1)}) %all-gather.26.cloned.1.call-update) | async-done | bytes 4718608 | tf_op jit(solution)/shard_map/all_gather | solution.py:107
  420.8 9.8 fusion.19
  430.6 79.6 %all-gather.22.cloned.1.call-done = bf16[1,3072,768]{2,1,0:T(8,128)(2,1)} async-done(((bf16[1,768,768]{2,1,0:T(8,128)(2,1)}), bf16[1,3072,768]{2,1,0:T(8,128)(2,1)}) %all-gather.22.cloned.1.call-update) | async-done | bytes 4718608 | tf_op jit(solution)/shard_map/all_gather | solution.py:108
  510.2 8.1 fusion.53
  519.3 3.7 all-to-all-start.1
  527.7 13.7 %all-gather.4 = bf16[4,192,16]{1,2,0:T(8,128)(2,1)S(1)} all-gather(bf16[1,192,16]{1,2,0:T(8,128)(2,1)S(1)} %convert_bitcast_fusion), channel_id=1, replica_groups=mesh['dp'=4,'expert'=8] {'dp'}, dimensions={0}, use_global_device_ids=true | all-gather | bytes 30720 | tf_op jit(solution)/shard_map/all_gather | solution.py:98
  542.0 3.3 gather_fusion.2
  555.0 5.4 all-to-all-start.2
  560.4 39.7 %all-gather.28.cloned.1.call-done = bf16[1,3072,768]{2,1,0:T(8,128)(2,1)} async-done(((bf16[1,768,768]{2,1,0:T(8,128)(2,1)}), bf16[1,3072,768]{2,1,0:T(8,128)(2,1)}) %all-gather.28.cloned.1.call-update) | async-done | bytes 4718608 | tf_op jit(solution)/shard_map/all_gather | solution.py:210
  600.1 11.5 %fusion.15 = bf16[8,2,40,3072]{3,2,0,1:T(8,128)(2,1)S(1)} fusion(f32[2,3072,8,40]{1,3,2,0:T(8,128)} %get-tuple-element.51, bf16[1,3072,768]{2,1,0:T(8,128)(2,1)} %all-gather.22.cloned.1.call-done, bf16[1,3072,768]{2,1,0:T(8,128)(2,1)} %all-gather.28.cloned.1.call-done, bf16[8,2,40,768]{3,2,1,0:T(8,128)(2,1)S(1)} %all-to-all-done.2), kind=kOutput, calls=%fused_computation.26 | convolution fusion | flops 3078094848 | bytes 22216704 | tf_op jit(solution)/shard_map/sekd,efd->sekf/dot_general | solution.py:217
  611.6 8.5 fusion.56
  621.2 3.7 all-to-all-start.3
  628.2 3.4 multiply_reduce_fusion.3
  631.6 7.9 all-to-all-done.3
  655.0 3.4 fusion.128
  659.8 5.0 fusion.67
  664.8 4.9 fusion.70
  669.7 3.4 fusion.85
  679.6 6.4 bitcast_convert_fusion
  686.1 6.6 bitcast_convert_fusion.1
  700.1 39.7 %all-reduce.6 = (f32[768,16]{0,1:T(8,128)S(1)}, f32[768]{0:T(1024)S(1)}, f32[768]{0:T(1024)S(1)}, f32[768]{0:T(1024)S(1)}, f32[768]{0:T(1024)S(1)}) all-reduce(f32[768,16]{0,1:T(8,128)S(1)} %fusion.130, f32[768]{0:T(1024)S(1)} %get-tuple-element.15, ...), channel_id=1, replica_groups=mesh['dp'=4,'expert'=8] {'dp','expert'}, use_global_device_ids=true, to_apply=%region_27.28 | all-reduce | flops 15360 | bytes 122880 | tf_op jit(solution)/shard_map/psum | solution.py:304
  744.1 124.4 %all-reduce.11.cloned.1.call-done = (f32[768,768]{1,0:T(8,128)}, f32[768,768]{1,0:T(8,128)}, f32[768,768]{1,0:T(8,128)}, f32[768,768]{1,0:T(8,128)}) async-done(((f32[768,768]{1,0:T(8,128)}, f32[768,768]{1,0:T(8,128)}, f32[768,768]{1,0:T(8,128)}, f32[768,768]{1,0:T(8,128)}), (f32[768,768]{1,0:T(8,128)}, f32[768,768]{1,0:T(8,128)}, f32[768,768]{1,0:T(8,128)}, ...) | async-done | bytes 9437200 | tf_op jit(solution)/shard_map/psum | solution.py:304
  876.2 79.9 %reduce-scatter.5.cloned.1.call-done = bf16[768,768]{1,0:T(8,128)(2,1)} async-done(((bf16[3072,768]{1,0:T(8,128)(2,1)}), bf16[768,768]{1,0:T(8,128)(2,1)}) %reduce-scatter.5.cloned.1.call-update) | async-done | bytes 1179664 | tf_op jit(solution)/shard_map/reduce_scatter | solution.py:236
  958.9 85.3 %reduce-scatter.3.cloned.1.call-done = bf16[192,3072]{1,0:T(8,128)(2,1)} async-done(((bf16[768,3072]{1,0:T(8,128)(2,1)}), bf16[192,3072]{1,0:T(8,128)(2,1)}) %reduce-scatter.3.cloned.1.call-update) | async-done | bytes 1179664 | tf_op jit(solution)/shard_map/reduce_scatter | solution.py:233
  (288 shorter events, 116.9 us)
Async XLA Ops:
  7.2 69.6 %all-gather.16.cloned.1.call-start = ((), (), s32[]{:S(2)}) async-start(), calls=%async_computation.7 | async-start | bytes 1474560 | tf_op jit(solution)/shard_map/all_gather | solution.py:94
  9.2 136.8 %all-gather.18.cloned.1.call-start = ((), (), s32[]{:S(2)}) async-start(), calls=%async_computation.8 | async-start | bytes 1474560 | tf_op jit(solution)/shard_map/all_gather | solution.py:95
  11.1 176.0 %all-gather.14.cloned.1.call-start = ((), (), s32[]{:S(2)}) async-start(), calls=%async_computation.6 | async-start | bytes 1474560 | tf_op jit(solution)/shard_map/all_gather | solution.py:96
  13.0 228.5 %all-gather.20.cloned.1.call-start = ((), (), s32[]{:S(2)}) async-start(), calls=%async_computation.9 | async-start | bytes 1474560 | tf_op jit(solution)/shard_map/all_gather | solution.py:97
  13.8 317.7 %all-gather.24.cloned.1.call-start = ((), (), s32[]{:S(2)}) async-start(), calls=%async_computation.13 | async-start | bytes 5898240 | tf_op jit(solution)/shard_map/all_gather | solution.py:105
  15.1 405.7 %all-gather.26.cloned.1.call-start = ((), (), s32[]{:S(2)}) async-start(), calls=%async_computation.14 | async-start | bytes 5898240 | tf_op jit(solution)/shard_map/all_gather | solution.py:107
  18.1 492.1 %all-gather.22.cloned.1.call-start = ((), (), s32[]{:S(2)}) async-start(), calls=%async_computation.12 | async-start | bytes 5898240 | tf_op jit(solution)/shard_map/all_gather | solution.py:108
  21.3 10.3 copy-start.61
  21.3 51.1 %copy-start.56 = (s32[1,256]{1,0:T(1,128)S(1)}, s32[1,256]{1,0:T(1,128)}, u32[]{:S(2)}) copy-start(s32[1,256]{1,0:T(1,128)} %param.18) | copy-start | bytes 3076
  21.3 578.8 %all-gather.28.cloned.1.call-start = ((), (), s32[]{:S(2)}) async-start(), calls=%async_computation.15 | async-start | bytes 5898240 | tf_op jit(solution)/shard_map/all_gather | solution.py:210
  22.5 50.1 %collective-permute-start = (bf16[1,768,768]{2,1,0:T(8,128)(2,1)}, bf16[1,768,768]{2,1,0:T(8,128)(2,1)}, u32[]{:S(2)}, u32[]{:S(2)}) collective-permute-start(bf16[1,768,768]{2,1,0:T(8,128)(2,1)} %convert_element_type.240), channel_id=1, source_target_pairs={{0,8},{8,0},{16,24},{24,16},{1,9},{9,1},{17,25},{25,17},{2,10},{10... | collective-permute-start | bytes 3538952 | tf_op jit(solution)/shard_map/ppermute | solution.py:24
  27.8 513.8 %copy-start.36 = (s32[512]{0:T(512)}, s32[512]{0:T(512)S(1)}, u32[]{:S(2)}) copy-start(s32[512]{0:T(512)S(1)} %fusion.89) | copy-start | bytes 6148
  72.0 115.1 %copy-start.29 = (f32[768]{0:T(1024)}, f32[768]{0:T(1024)S(1)}, u32[]{:S(2)}) copy-start(f32[768]{0:T(1024)S(1)} %convert_element_type.227) | copy-start | bytes 9220
  72.0 171.6 %copy-start.31 = (f32[768]{0:T(1024)}, f32[768]{0:T(1024)S(1)}, u32[]{:S(2)}) copy-start(f32[768]{0:T(1024)S(1)} %convert_element_type.249) | copy-start | bytes 9220
  72.3 114.8 %copy-start.34 = (f32[256]{0:T(256)}, f32[256]{0:T(256)S(1)}, u32[]{:S(2)}) copy-start(f32[256]{0:T(256)S(1)} %fusion.102) | copy-start | bytes 3076
  72.5 116.6 %copy-start.27 = (pred[256,256]{0,1:T(8,128)(4,1)}, pred[256,256]{0,1:T(8,128)(4,1)S(1)}, u32[]{:S(2)}) copy-start(pred[256,256]{0,1:T(8,128)(4,1)S(1)} %fusion.84) | copy-start | bytes 196612
  76.8 175.2 %collective-permute-start.1 = (bf16[2,768,768]{2,1,0:T(8,128)(2,1)}, bf16[2,768,768]{2,1,0:T(8,128)(2,1)}, u32[]{:S(2)}, u32[]{:S(2)}) collective-permute-start(bf16[2,768,768]{2,1,0:T(8,128)(2,1)} %get-tuple-element.40), channel_id=1, source_target_pairs={{0,16},{8,24},{16,0},{24,8},{1,17},{9,25},{17,1},{25,9},{2,18},{10... | collective-permute-start | bytes 7077896 | tf_op jit(solution)/shard_map/ppermute | solution.py:24
  78.8 110.3 %copy-start.21 = (bf16[256,768]{0,1:T(8,128)(2,1)}, bf16[256,768]{0,1:T(8,128)(2,1)S(1)}, u32[]{:S(2)}) copy-start(bf16[256,768]{0,1:T(8,128)(2,1)S(1)} %copy.86) | copy-start | bytes 1179652
  148.0 41.8 %copy-start.22 = (bf16[256,768]{0,1:T(8,128)(2,1)}, bf16[256,768]{0,1:T(8,128)(2,1)S(1)}, u32[]{:S(2)}) copy-start(bf16[256,768]{0,1:T(8,128)(2,1)S(1)} %copy.87) | copy-start | bytes 1179652
  192.2 51.4 %copy-start.18 = (bf16[12,64,256]{2,1,0:T(8,128)(2,1)}, bf16[12,64,256]{2,1,0:T(8,128)(2,1)S(1)}, u32[]{:S(2)}) copy-start(bf16[12,64,256]{2,1,0:T(8,128)(2,1)S(1)} %fusion.63) | copy-start | bytes 1179652
  248.0 18.5 %all-to-all-start = ((bf16[8,2,40,768]{3,2,1,0:T(8,128)(2,1)}), bf16[8,2,40,768]{3,2,1,0:T(8,128)(2,1)S(1)}, u32[]{:S(2)}, u32[]{:S(2)}) async-start(bf16[8,2,40,768]{3,2,1,0:T(8,128)(2,1)} %bitcast.20), calls=%async_computation | async-start | bytes 1966080 | tf_op jit(solution)/shard_map/all_to_all | solution.py:183
  266.5 164.0 %copy-start.24 = (bf16[8,2,40,768]{3,2,1,0:T(8,128)(2,1)}, bf16[8,2,40,768]{3,2,1,0:T(8,128)(2,1)S(1)}, u32[]{:S(2)}) copy-start(bf16[8,2,40,768]{3,2,1,0:T(8,128)(2,1)S(1)} %all-to-all-done) | copy-start | bytes 2949124
  519.3 26.3 %all-to-all-start.1 = ((bf16[8,2,40,768]{3,2,1,0:T(8,128)(2,1)}), bf16[8,2,40,768]{3,2,1,0:T(8,128)(2,1)S(1)}, u32[]{:S(2)}, u32[]{:S(2)}) async-start(bf16[8,2,40,768]{3,2,1,0:T(8,128)(2,1)} %copy.94), calls=%async_computation.1 | async-start | bytes 1966080 | tf_op jit(solution)/shard_map/all_to_all | solution.py:191
  555.0 45.1 %all-to-all-start.2 = ((bf16[8,2,40,768]{3,2,1,0:T(8,128)(2,1)}), bf16[8,2,40,768]{3,2,1,0:T(8,128)(2,1)S(1)}, u32[]{:S(2)}, u32[]{:S(2)}) async-start(bf16[8,2,40,768]{3,2,1,0:T(8,128)(2,1)} %multiply_convert_fusion), calls=%async_computation.2 | async-start | bytes 1966080 | tf_op jit(solution)/shard_map/all_to_all | solution.py:216
  600.1 11.5 %copy-start.25 = (bf16[8,2,40,768]{3,2,1,0:T(8,128)(2,1)}, bf16[8,2,40,768]{3,2,1,0:T(8,128)(2,1)S(1)}, u32[]{:S(2)}) copy-start(bf16[8,2,40,768]{3,2,1,0:T(8,128)(2,1)S(1)} %all-to-all-done.2) | copy-start | bytes 2949124
  621.2 18.3 %all-to-all-start.3 = ((bf16[8,2,40,768]{3,2,1,0:T(8,128)(2,1)}), bf16[8,2,40,768]{3,2,1,0:T(8,128)(2,1)S(1)}, u32[]{:S(2)}, u32[]{:S(2)}) async-start(bf16[8,2,40,768]{3,2,1,0:T(8,128)(2,1)} %copy.100), calls=%async_computation.3 | async-start | bytes 1966080 | tf_op jit(solution)/shard_map/all_to_all | solution.py:240
  624.8 243.7 %all-reduce.11.cloned.1.call-start = ((), (), s32[]{:S(2)}) async-start(), calls=%async_computation.16 | async-start | bytes 18874368 | tf_op jit(solution)/shard_map/psum | solution.py:304
  679.3 276.7 %reduce-scatter.5.cloned.1.call-start = ((), (), s32[]{:S(2)}) async-start(), calls=%async_computation.11 | async-start | bytes 5898240 | tf_op jit(solution)/shard_map/reduce_scatter | solution.py:236
  686.0 358.2 %reduce-scatter.3.cloned.1.call-start = ((), (), s32[]{:S(2)}) async-start(), calls=%async_computation.10 | async-start | bytes 5898240 | tf_op jit(solution)/shard_map/reduce_scatter | solution.py:233
  697.5 45.5 %copy-start.4 = (f32[256,768]{1,0:T(8,128)S(1)}, f32[256,768]{1,0:T(8,128)}, u32[]{:S(2)}) copy-start(f32[256,768]{1,0:T(8,128)} %copy-done.3) | copy-start | bytes 2359300
  697.5 45.5 %copy-start.7 = (bf16[256,768]{1,0:T(8,128)(2,1)S(1)}, bf16[256,768]{1,0:T(8,128)(2,1)}, u32[]{:S(2)}) copy-start(bf16[256,768]{1,0:T(8,128)(2,1)} %param.33) | copy-start | bytes 1179652
  697.5 45.5 %copy-start.43 = (f32[256]{0:T(256)S(1)}, f32[256]{0:T(256)}, u32[]{:S(2)}) copy-start(f32[256]{0:T(256)} %copy-done.42) | copy-start | bytes 3076
  (48 other events, 215.2 us)
Sparse Core Ops, SparseCore 0:
  10.1 43.7 all-gather.15
  56.1 89.8 all-gather.17
  148.2 38.8 all-gather.13
  189.1 52.3 all-gather.19
  242.9 88.6 all-gather.23
  333.0 87.7 all-gather.25
  422.4 87.7 all-gather.21
  511.8 88.2 all-gather.27
  679.5 189.0 all-reduce.10
  870.7 85.3 reduce-scatter.4
  958.3 85.7 reduce-scatter.2
